TPU v7x, 128 devices: a whole 4x4x4 slice. The times are simulated.
128 devices in a mesh: grp: 16 (over z, x), reg: 8 (over y, core).
Axes of the slice: x: 4, y: 4, z: 4, core: 2. Of those that a mesh axis runs over, the one named last changes fastest.
Arguments:
- orbitals: bfloat16 [8, 16, 512, 1024], P('reg', 'grp'), may hold values from -6 to 6
- occupied: bfloat16 [8, 16, 8, 512], P('reg', 'grp'), may hold values from -0.59765625 to 0.59765625
- panel_index: int32 [128], replicated, may hold values from 0 to 1023, as said below
- screening: bfloat16 [896, 512, 512], P(('grp', 'reg')), may hold values from -0.25 to 0.25
- block_region: int32 [896, 1], P(('grp', 'reg')), may hold values from 0 to 7; in each aligned block of 7 rows (0 to 6, 7 to 13, ...) at most 2 rows name the same one
- block_row: int32 [896], P(('grp', 'reg')), may hold values from 0 to 15
- block_col: int32 [896], P(('grp', 'reg')), may hold values from 0 to 15
Outputs:
- sigma: float32 [8, 128, 128], P('reg')
Inputs may be any that keep to these rules, and one draw needn't show every extreme that they name: `panel_index`: the 128 indices are distinct. Among the 7 blocks of one device (aligned rows of block_region), at most 2 name the same region.
All inputs are finite; a program needn't handle non-finite values.
Results may differ from a plain program's by a relative error of at most 0.0054.
Values may be sent and summed in bfloat16 or wider, within the bound.
A program may use at most 192 MiB of HBM per device.

v0:
```python
import jax
import jax.numpy as jnp
from jax import lax
from jax.sharding import PartitionSpec as P

CAP = 2


def form_pairs(orbital_rows, occupied_rows):
    pairs = orbital_rows[..., :, None, :].astype(jnp.float32) * jnp.swapaxes(occupied_rows, -1, -2)[
        ..., None
    ].astype(jnp.float32)
    return pairs.astype(jnp.bfloat16)


def shards(orbitals, occupied, panel_index, screening, block_region, block_row, block_col):
    regions = lax.axis_size("reg")
    panel_orbs = jnp.take(orbitals[0], panel_index, axis=2)
    occ_rows = occupied[0]
    grid_points = screening.shape[1]
    panel_width = panel_orbs.shape[2]
    occ_count = occ_rows.shape[1]
    held_count = screening.shape[0]
    slot_count = regions * CAP
    destination = block_region[:, 0]
    membership = (destination[:, None] == jnp.arange(regions, dtype=jnp.int32)[None, :]).astype(
        jnp.int32
    )
    earlier = jnp.cumsum(membership, axis=0) - membership
    slot_of = destination * CAP + jnp.sum(earlier * membership, axis=1)
    matched = (slot_of[None, :] == jnp.arange(slot_count, dtype=jnp.int32)[:, None]).astype(
        jnp.int32
    )
    filled = jnp.sum(matched, axis=1)
    source = jnp.sum(matched * jnp.arange(held_count, dtype=jnp.int32)[None, :], axis=1)
    outgoing = jnp.take(screening, source, axis=0) * filled[:, None, None].astype(jnp.bfloat16)
    labels = jnp.stack(
        [jnp.take(block_row, source) * filled, jnp.take(block_col, source) * filled, filled], axis=1
    )
    gathered = lax.all_gather(form_pairs(panel_orbs, occ_rows), "grp", axis=0, tiled=True)

    def select_pairs(indices):
        return jnp.take(gathered, indices, axis=0)

    incoming, arrived = (
        lax.all_to_all(
            outgoing.reshape(regions, CAP, grid_points, grid_points),
            "reg",
            split_axis=0,
            concat_axis=0,
            tiled=True,
        ),
        lax.all_to_all(
            labels.reshape(regions, CAP, 3), "reg", split_axis=0, concat_axis=0, tiled=True
        ),
    )
    incoming = incoming.reshape(slot_count, grid_points, grid_points)
    arrived = arrived.reshape(slot_count, 3)
    col_pairs = select_pairs(arrived[:, 1]).reshape(
        slot_count, grid_points, occ_count * panel_width
    )
    screened = jnp.einsum(
        "spq,sqc->spc", incoming, col_pairs, preferred_element_type=jnp.float32
    ).astype(jnp.bfloat16)
    row_pairs = select_pairs(arrived[:, 0]).reshape(
        slot_count, grid_points * occ_count, panel_width
    )
    partial_sigma = jnp.einsum(
        "sri,srj->ij",
        row_pairs,
        screened.reshape(slot_count, grid_points * occ_count, panel_width),
        preferred_element_type=jnp.float32,
    )
    sigma = lax.psum(partial_sigma, "grp")
    return sigma[None]


def solution(mesh):
    in_specs = (
        P("reg", "grp", None, None),
        P("reg", "grp", None, None),
        P(),
        P(("grp", "reg"), None, None),
        P(("grp", "reg"), None),
        P(("grp", "reg")),
        P(("grp", "reg")),
    )
    out_specs = P("reg", None, None)
    return jax.shard_map(shards, mesh=mesh, in_specs=in_specs, out_specs=out_specs, check_vma=False)
```

profile of v0, /device:TPU:0, one launch (start us, length us, event | category | flops | bytes accessed | tf_op | source)
XLA Modules:
  0.0 339.5 jit_solution(4951172310689396512)
XLA Ops:
  6.5 0.7 compare_and_fusion.4
  7.9 0.7 convert_bitcast_fusion.1
  8.7 1.5 copy.26
  10.2 0.8 gather_fusion
  11.3 1.6 multiply_convert_fusion
  12.9 0.7 fusion.8
  13.6 0.8 select_reduce_fusion.1
  14.5 0.7 multiply_add_fusion
  15.9 1.3 gather_fusion.2
  17.5 0.7 copy.24
  18.2 4.6 %all-to-all-start = ((s32[8,2,3]{2,1,0:T(2,128)}), s32[8,2,3]{2,1,0:T(2,128)S(1)}, u32[]{:S(2)}, u32[]{:S(2)}) async-start(s32[8,2,3]{2,1,0:T(2,128)} %copy.24), calls=%async_computation | async-start | bytes 16384 | tf_op jit(solution)/shard_map/all_to_all | solution.py:53
  23.0 6.9 %gather_fusion.1 = bf16[16,512,512]{2,1,0:T(8,128)(2,1)} fusion(bf16[7,512,512]{2,1,0:T(8,128)(2,1)} %param.14, s32[1024]{0:T(1024)S(1)} %pad_clamp_fusion.1), kind=kCustom, calls=%fused_computation.5 | custom fusion | bytes 16777280 | tf_op jit(solution)/shard_map/jit(_take)/gather | solution.py:36
  29.9 7.4 %select_multiply_fusion = bf16[8,2,512,512]{3,2,1,0:T(8,128)(2,1)} fusion(bf16[8,2,512,512]{3,2,1,0:T(8,128)(2,1)} %bitcast.40, pred[8,2]{1,0:T(8,128)(4,1)S(1)} %compare_and_fusion, bf16[8,2]{1,0:T(8,128)(2,1)S(1)} %convert_element_type.65), kind=kLoop, calls=%fused_computation.13 | loop fusion | flops 8388608 | bytes 16777264 | tf_op jit(solution)/shard_map/mul | solution.py:36
  37.4 5.0 %all-to-all-start.1 = ((bf16[8,2,512,512]{3,2,1,0:T(8,128)(2,1)}), bf16[8,2,512,512]{3,2,1,0:T(8,128)(2,1)}, u32[]{:S(2)}, u32[]{:S(2)}) async-start(bf16[8,2,512,512]{3,2,1,0:T(8,128)(2,1)} %select_multiply_fusion), calls=%async_computation.1 | async-start | bytes 16777216 | tf_op jit(solution)/shard_map/all_to_all | solution.py:46
  42.9 84.2 %all-gather.2.cloned.1.call-done = bf16[16,512,8,128]{3,2,1,0:T(8,128)(2,1)} async-done(((bf16[1,512,8,128]{3,2,1,0:T(8,128)(2,1)}), bf16[16,512,8,128]{3,2,1,0:T(8,128)(2,1)}) %all-gather.2.cloned.1.call-update) | async-done | bytes 16777232 | tf_op jit(solution)/shard_map/all_gather | solution.py:40
  127.0 13.0 %gather_fusion.5 = bf16[16,512,8,128]{3,2,1,0:T(8,128)(2,1)} fusion(bf16[16,512,8,128]{3,2,1,0:T(8,128)(2,1)} %all-gather.2.cloned.1.call-done, s32[1024]{0:T(1024)S(1)} %pad_clamp_fusion), kind=kCustom, calls=%fused_computation.3.clone | custom fusion | bytes 33554496 | tf_op jit(solution)/shard_map/jit(_take)/gather | solution.py:43
  140.0 14.2 %broadcast_select_fusion = bf16[16,512,8,128]{3,2,1,0:T(8,128)(2,1)} fusion(bf16[16,512,8,128]{3,2,1,0:T(8,128)(2,1)} %gather_fusion.5, pred[16]{0:T(512)(128)(4,1)S(1)} %compare_and_fusion.1), kind=kLoop, calls=%fused_computation.9 | loop fusion | flops 8388608 | bytes 33554448 | tf_op jit(solution)/shard_map/jit(_take)/select_n | solution.py:43
  154.2 25.3 %reshape.130 = bf16[16,512,1024]{2,1,0:T(8,128)(2,1)} reshape(bf16[16,512,8,128]{3,2,1,0:T(8,128)(2,1)} %broadcast_select_fusion) | data formatting | bytes 33554432 | tf_op jit(solution)/shard_map/reshape | solution.py:59
  179.5 17.0 %convolution_convert_fusion = bf16[16,512,1024]{2,1,0:T(8,128)(2,1)} fusion(bf16[16,512,512]{2,1,0:T(8,128)(2,1)} %bitcast.12, bf16[16,512,1024]{2,1,0:T(8,128)(2,1)} %reshape.130), kind=kOutput, calls=%fused_computation.11 | convolution fusion | flops 8598323200 | bytes 41943040 | tf_op jit(solution)/shard_map/spq,sqc->spc/dot_general | solution.py:62
  196.4 25.3 %reshape.131 = bf16[16,4096,128]{2,1,0:T(8,128)(2,1)} reshape(bf16[16,512,1024]{2,1,0:T(8,128)(2,1)} %convolution_convert_fusion) | data formatting | bytes 33554432 | tf_op jit(solution)/shard_map/reshape | solution.py:71
  221.7 13.0 %gather_fusion.4 = bf16[16,512,8,128]{3,2,1,0:T(8,128)(2,1)} fusion(bf16[16,512,8,128]{3,2,1,0:T(8,128)(2,1)} %all-gather.2.cloned.1.call-done, s32[1024]{0:T(1024)S(1)} %pad_clamp_fusion.2), kind=kCustom, calls=%fused_computation.1.clone | custom fusion | bytes 33554496 | tf_op jit(solution)/shard_map/jit(_take)/gather | solution.py:43
  234.7 16.3 %fusion.5 = f32[1,128,128]{2,1,0:T(8,128)} fusion(bf16[16,4096,128]{2,1,0:T(8,128)(2,1)} %reshape.131, bf16[16,512,8,128]{3,2,1,0:T(8,128)(2,1)} %gather_fusion.4, pred[16]{0:T(512)(128)(4,1)S(1)} %compare_and_fusion.2), kind=kOutput, calls=%fused_computation.15 | convolution fusion | flops 2155872256 | bytes 33619984 | tf_op jit(solution)/shard_map/sri,srj->ij/dot_general | solution.py:68
  251.0 80.2 %all-reduce.2.cloned.1.call-done = f32[1,128,128]{2,1,0:T(8,128)} async-done(((f32[1,128,128]{2,1,0:T(8,128)}), f32[1,128,128]{2,1,0:T(8,128)}) %all-reduce.2.cloned.1.call-update) | async-done | bytes 65552 | tf_op jit(solution)/shard_map/psum | solution.py:74
  331.2 1.5 copy.35
  (39 shorter events, 2.8 us)
Async XLA Ops:
  6.5 8.7 %copy-start = (s32[7]{0:T(128)S(1)}, s32[7]{0:T(128)}, u32[]{:S(2)}) copy-start(s32[7]{0:T(128)} %param.17) | copy-start | bytes 88
  6.5 120.5 %all-gather.2.cloned.1.call-start = ((), (), s32[]{:S(2)}) async-start(), calls=%async_computation.2 | async-start | bytes 17825792 | tf_op jit(solution)/shard_map/all_gather | solution.py:40
  18.2 19.1 %all-to-all-start = ((s32[8,2,3]{2,1,0:T(2,128)}), s32[8,2,3]{2,1,0:T(2,128)S(1)}, u32[]{:S(2)}, u32[]{:S(2)}) async-start(s32[8,2,3]{2,1,0:T(2,128)} %copy.24), calls=%async_computation | async-start | bytes 16384 | tf_op jit(solution)/shard_map/all_to_all | solution.py:53
  37.4 142.1 %all-to-all-start.1 = ((bf16[8,2,512,512]{3,2,1,0:T(8,128)(2,1)}), bf16[8,2,512,512]{3,2,1,0:T(8,128)(2,1)}, u32[]{:S(2)}, u32[]{:S(2)}) async-start(bf16[8,2,512,512]{3,2,1,0:T(8,128)(2,1)} %select_multiply_fusion), calls=%async_computation.1 | async-start | bytes 16777216 | tf_op jit(solution)/shard_map/all_to_all | solution.py:46
  42.3 288.9 %all-reduce.2.cloned.1.call-start = ((), (), s32[]{:S(2)}) async-start(), calls=%async_computation.3 | async-start | bytes 131072 | tf_op jit(solution)/shard_map/psum | solution.py:74
  221.7 111.0 %copy-start.1 = (s32[7]{0:T(128)S(1)}, s32[7]{0:T(128)}, u32[]{:S(2)}) copy-start(s32[7]{0:T(128)} %param.17) | copy-start | bytes 88
Sparse Core Ops, SparseCore 0:
  13.0 113.9 all-gather.1
  251.1 80.0 all-reduce.1
where the time goes:
time: 341 us; the launch traced here: 340 us
  waiting for transfers between devices  164 us (48%)
  local copies, waits for them, and re-layouts  90.9 us (27%)
  matrix products  33.3 us (10%)
  other arithmetic  27.7 us (8%)
  between operations  13.5 us (4%)
  starting transfers between devices  9.74 us (3%)
    all_gather x1, waiting for transfers between devices, shards(): lax.all_gather(form_pairs(panel_orbs, occ_rows), 'grp', axis=0, tiled=True)  84.2 us
    psum x1, waiting for transfers between devices, shards(): sigma = lax.psum(partial_sigma, 'grp')  80.2 us
    gather x2, local copies, waits for them, and re-layouts, select_pairs(): return jnp.take(gathered, indices, axis=0)  25.9 us
    reshape x1, local copies, waits for them, and re-layouts, shards(): select_pairs(arrived[:, 1])  25.3 us
    reshape x1, local copies, waits for them, and re-layouts, shards(): screened.reshape(slot_count, grid_points * occ_count, panel_width)  25.3 us
    dot_general x1, matrix products, shards(): jnp.einsum('spq,sqc->spc', incoming, col_pairs, preferred_element_type=jn...  17 us
    dot_general x1, matrix products, shards(): jnp.einsum('sri,srj->ij', row_pairs, screened.reshape(slot_count, grid_po...  16.3 us
    select_n x3, other arithmetic, select_pairs(): return jnp.take(gathered, indices, axis=0)  14.2 us
  transfers between devices with their start and end apart: 4, of which 2 were waited for; matrix products, arithmetic and copies ran while one was open for 21% of the time, Pallas kernels for 0%

commit v1 on v0

--- a/solution.py
+++ b/solution.py
@@ -37,7 +37,12 @@
     labels = jnp.stack(
         [jnp.take(block_row, source) * filled, jnp.take(block_col, source) * filled, filled], axis=1
     )
-    gathered = lax.all_gather(form_pairs(panel_orbs, occ_rows), "grp", axis=0, tiled=True)
+    gathered = jnp.concatenate(
+        lax.all_to_all(
+            jnp.stack([form_pairs(panel_orbs, occ_rows)] * lax.axis_size("grp")), "grp", 0, 0
+        ),
+        axis=0,
+    )
 
     def select_pairs(indices):
         return jnp.take(gathered, indices, axis=0)

time: 341 us -> 534 us (1.57)
  waiting for transfers between devices: 164 us -> 344 us
  starting transfers between devices: 9.74 us -> 17.7 us
  local copies, waits for them, and re-layouts: 90.9 us -> 96.7 us
    all_to_all x0 -> x1, waiting for transfers between devices: none -> 239 us  [shards(): lax.all_to_all(jnp.stack([form_pairs(panel_orbs, occ_rows)] * lax.axis_si...]
    all_gather x1 -> x0, waiting for transfers between devices: 84.2 us -> none  [shards(): lax.all_gather(form_pairs(panel_orbs, occ_rows), 'grp', axis=0, tiled=True)]
    all_to_all x1, waiting for transfers between devices: 0.01 us -> 28.7 us  [shards(): lax.all_to_all(outgoing.reshape(regions, CAP, grid_points, grid_points),...]
    all_to_all x0 -> x1, starting transfers between devices: none -> 7.93 us  [shards(): lax.all_to_all(jnp.stack([form_pairs(panel_orbs, occ_rows)] * lax.axis_si...]
    another operation x0 -> x1, local copies, waits for them, and re-layouts: none -> 6.14 us  [shards(): jnp.stack([form_pairs(panel_orbs, occ_rows)] * lax.axis_size('grp'))]
  transfers between devices with their start and end apart: 4 -> 4, of which waited for: 2 -> 3; matrix products, arithmetic and copies ran while one was open for 21% -> 16% of each run, Pallas kernels for 0% -> 0%
where the time goes in v1:
time: 534 us; the launch traced here: 532 us
  waiting for transfers between devices  344 us (64%)
  local copies, waits for them, and re-layouts  96.7 us (18%)
  matrix products  33.2 us (6%)
  other arithmetic  26.8 us (5%)
  starting transfers between devices  17.7 us (3%)
  between operations  13.5 us (3%)
    all_to_all x1, waiting for transfers between devices, shards(): lax.all_to_all(jnp.stack([form_pairs(panel_orbs, occ_rows)] * lax.axis_si...  239 us
    psum x1, waiting for transfers between devices, shards(): sigma = lax.psum(partial_sigma, 'grp')  76 us
    all_to_all x1, waiting for transfers between devices, shards(): lax.all_to_all(outgoing.reshape(regions, CAP, grid_points, grid_points),...  28.7 us
    gather x2, local copies, waits for them, and re-layouts, select_pairs(): return jnp.take(gathered, indices, axis=0)  25.9 us
    reshape x1, local copies, waits for them, and re-layouts, shards(): screened.reshape(slot_count, grid_points * occ_count, panel_width)  25.3 us
    reshape x1, local copies, waits for them, and re-layouts, shards(): select_pairs(arrived[:, 1])  25.3 us
    dot_general x1, matrix products, shards(): jnp.einsum('spq,sqc->spc', incoming, col_pairs, preferred_element_type=jn...  16.9 us
    dot_general x1, matrix products, shards(): jnp.einsum('sri,srj->ij', row_pairs, screened.reshape(slot_count, grid_po...  16.3 us
  transfers between devices with their start and end apart: 4, of which 3 were waited for; matrix products, arithmetic and copies ran while one was open for 16% of the time, Pallas kernels for 0%

profile of v1, /device:TPU:0, one launch (start us, length us, event | category | flops | bytes accessed | tf_op | source)
XLA Modules:
  0.0 531.7 jit_solution(8971619921990577692)
XLA Ops:
  6.5 0.7 fusion.8
  7.3 0.8 select_reduce_fusion.1
  9.6 1.3 gather_fusion.2
  11.2 0.7 copy.24
  11.9 4.6 all-to-all-start.1
  18.6 1.5 copy.26
  20.1 0.8 gather_fusion
  21.2 0.7 multiply_convert_fusion
  21.9 6.1 %stack.10 = bf16[16,1,512,8,128]{4,3,2,1,0:T(8,128)(2,1)} broadcast(bf16[512,8,128]{2,1,0:T(8,128)(2,1)S(1)} %multiply_convert_fusion), dimensions={2,3,4} | broadcast | bytes 17825792 | tf_op jit(solution)/shard_map/stack | solution.py:42
  28.1 7.9 %all-to-all-start = ((bf16[16,1,512,8,128]{4,3,2,1,0:T(8,128)(2,1)}), bf16[16,1,512,8,128]{4,3,2,1,0:T(8,128)(2,1)}, u32[]{:S(2)}, u32[]{:S(2)}) async-start(bf16[16,1,512,8,128]{4,3,2,1,0:T(8,128)(2,1)} %stack.10), calls=%async_computation | async-start | bytes 33554432 | tf_op jit(solution)/shard_map/all_to_all | solution.py:41
  36.2 6.7 %gather_fusion.1 = bf16[16,512,512]{2,1,0:T(8,128)(2,1)} fusion(bf16[7,512,512]{2,1,0:T(8,128)(2,1)} %param.14, s32[1024]{0:T(1024)S(1)} %pad_clamp_fusion.1), kind=kCustom, calls=%fused_computation.5 | custom fusion | bytes 16777280 | tf_op jit(solution)/shard_map/jit(_take)/gather | solution.py:36
  42.9 7.4 %select_multiply_fusion = bf16[8,2,512,512]{3,2,1,0:T(8,128)(2,1)} fusion(bf16[8,2,512,512]{3,2,1,0:T(8,128)(2,1)} %bitcast.41, pred[8,2]{1,0:T(8,128)(4,1)S(1)} %compare_and_fusion, bf16[8,2]{1,0:T(8,128)(2,1)S(1)} %convert_element_type.64), kind=kLoop, calls=%fused_computation.13 | loop fusion | flops 8388608 | bytes 16777264 | tf_op jit(solution)/shard_map/mul | solution.py:36
  50.3 238.9 %all-to-all-done = bf16[16,1,512,8,128]{4,3,2,1,0:T(8,128)(2,1)} async-done(((bf16[16,1,512,8,128]{4,3,2,1,0:T(8,128)(2,1)}), bf16[16,1,512,8,128]{4,3,2,1,0:T(8,128)(2,1)}, u32[]{:S(2)}, u32[]{:S(2)}) %all-to-all-start) | async-done | bytes 16777248 | tf_op jit(solution)/shard_map/all_to_all | solution.py:41
  289.2 5.0 all-to-all-start.2
  294.7 13.0 %gather_fusion.5 = bf16[16,512,8,128]{3,2,1,0:T(8,128)(2,1)} fusion(bf16[16,512,8,128]{3,2,1,0:T(8,128)(2,1)} %bitcast.8, s32[1024]{0:T(1024)S(1)} %pad_clamp_fusion), kind=kCustom, calls=%fused_computation.3.clone | custom fusion | bytes 33554496 | tf_op jit(solution)/shard_map/jit(_take)/gather | solution.py:48
  307.6 12.9 %gather_fusion.4 = bf16[16,512,8,128]{3,2,1,0:T(8,128)(2,1)} fusion(bf16[16,512,8,128]{3,2,1,0:T(8,128)(2,1)} %bitcast.8, s32[1024]{0:T(1024)S(1)} %pad_clamp_fusion.2), kind=kCustom, calls=%fused_computation.1.clone | custom fusion | bytes 33554496 | tf_op jit(solution)/shard_map/jit(_take)/gather | solution.py:48
  320.6 14.2 %broadcast_select_fusion = bf16[16,512,8,128]{3,2,1,0:T(8,128)(2,1)} fusion(bf16[16,512,8,128]{3,2,1,0:T(8,128)(2,1)} %gather_fusion.5, pred[16]{0:T(512)(128)(4,1)S(1)} %compare_and_fusion.1), kind=kLoop, calls=%fused_computation.9 | loop fusion | flops 8388608 | bytes 33554448 | tf_op jit(solution)/shard_map/jit(_take)/select_n | solution.py:48
  334.7 25.3 %reshape.132 = bf16[16,512,1024]{2,1,0:T(8,128)(2,1)} reshape(bf16[16,512,8,128]{3,2,1,0:T(8,128)(2,1)} %broadcast_select_fusion) | data formatting | bytes 33554432 | tf_op jit(solution)/shard_map/reshape | solution.py:64
  360.0 28.7 %all-to-all-done.2 = bf16[8,2,512,512]{3,2,1,0:T(8,128)(2,1)} async-done(((bf16[8,2,512,512]{3,2,1,0:T(8,128)(2,1)}), bf16[8,2,512,512]{3,2,1,0:T(8,128)(2,1)}, u32[]{:S(2)}, u32[]{:S(2)}) %all-to-all-start.2) | async-done | bytes 8388640 | tf_op jit(solution)/shard_map/all_to_all | solution.py:51
  388.8 16.9 %convolution_convert_fusion = bf16[16,512,1024]{2,1,0:T(8,128)(2,1)} fusion(bf16[16,512,512]{2,1,0:T(8,128)(2,1)} %bitcast.13, bf16[16,512,1024]{2,1,0:T(8,128)(2,1)} %reshape.132), kind=kOutput, calls=%fused_computation.11 | convolution fusion | flops 8598323200 | bytes 41943040 | tf_op jit(solution)/shard_map/spq,sqc->spc/dot_general | solution.py:67
  405.7 25.3 %reshape.133 = bf16[16,4096,128]{2,1,0:T(8,128)(2,1)} reshape(bf16[16,512,1024]{2,1,0:T(8,128)(2,1)} %convolution_convert_fusion) | data formatting | bytes 33554432 | tf_op jit(solution)/shard_map/reshape | solution.py:76
  431.0 16.3 %fusion.5 = f32[1,128,128]{2,1,0:T(8,128)} fusion(bf16[16,4096,128]{2,1,0:T(8,128)(2,1)} %reshape.133, bf16[16,512,8,128]{3,2,1,0:T(8,128)(2,1)} %gather_fusion.4, pred[16]{0:T(512)(128)(4,1)S(1)} %compare_and_fusion.2), kind=kOutput, calls=%fused_computation.15 | convolution fusion | flops 2155872256 | bytes 33619984 | tf_op jit(solution)/shard_map/sri,srj->ij/dot_general | solution.py:73
  447.4 76.0 %all-reduce.2.cloned.1.call-done = f32[1,128,128]{2,1,0:T(8,128)} async-done(((f32[1,128,128]{2,1,0:T(8,128)}), f32[1,128,128]{2,1,0:T(8,128)}) %all-reduce.2.cloned.1.call-update) | async-done | bytes 65552 | tf_op jit(solution)/shard_map/psum | solution.py:79
  523.3 1.5 copy.35
  (39 shorter events, 4.8 us)
Async XLA Ops:
  6.5 2.4 copy-start
  11.9 10.0 %all-to-all-start.1 = ((s32[8,2,3]{2,1,0:T(2,128)}), s32[8,2,3]{2,1,0:T(2,128)S(1)}, u32[]{:S(2)}, u32[]{:S(2)}) async-start(s32[8,2,3]{2,1,0:T(2,128)} %copy.24), calls=%async_computation.1 | async-start | bytes 16384 | tf_op jit(solution)/shard_map/all_to_all | solution.py:58
  28.1 261.1 %all-to-all-start = ((bf16[16,1,512,8,128]{4,3,2,1,0:T(8,128)(2,1)}), bf16[16,1,512,8,128]{4,3,2,1,0:T(8,128)(2,1)}, u32[]{:S(2)}, u32[]{:S(2)}) async-start(bf16[16,1,512,8,128]{4,3,2,1,0:T(8,128)(2,1)} %stack.10), calls=%async_computation | async-start | bytes 33554432 | tf_op jit(solution)/shard_map/all_to_all | solution.py:41
  289.2 99.6 %all-to-all-start.2 = ((bf16[8,2,512,512]{3,2,1,0:T(8,128)(2,1)}), bf16[8,2,512,512]{3,2,1,0:T(8,128)(2,1)}, u32[]{:S(2)}, u32[]{:S(2)}) async-start(bf16[8,2,512,512]{3,2,1,0:T(8,128)(2,1)} %select_multiply_fusion), calls=%async_computation.2 | async-start | bytes 16777216 | tf_op jit(solution)/shard_map/all_to_all | solution.py:51
  294.2 229.2 %all-reduce.2.cloned.1.call-start = ((), (), s32[]{:S(2)}) async-start(), calls=%async_computation.3 | async-start | bytes 131072 | tf_op jit(solution)/shard_map/psum | solution.py:79
  405.7 119.1 %copy-start.1 = (s32[7]{0:T(128)S(1)}, s32[7]{0:T(128)}, u32[]{:S(2)}) copy-start(s32[7]{0:T(128)} %param.17) | copy-start | bytes 88
Sparse Core Ops, SparseCore 0:
  447.5 75.8 all-reduce.1
